TPU v7x, 128 devices: a whole 4x4x4 slice. The times are simulated.
128 devices in a mesh: row: 32 (over z, y, core), col: 4 (over x).
Axes of the slice: x: 4, y: 4, z: 4, core: 2. Of those that a mesh axis runs over, the one named last changes fastest.
Arguments:
- tokens: bfloat16 [16384, 2048], P('row', 'col'), may hold values from -6 to 6
- cotangent: bfloat16 [16384, 2048], P('row', 'col'), may hold values from -6 to 6
- destination: int32 [16384], P('row'), may hold values from 0 to 16383, as said below
- segment_ids: int32 [16384], P('row'), may hold values from 0 to 7, as said below
- attn_gain: float32 [2048], replicated, may hold values from 0.5 to 1.5
- w_query: bfloat16 [2048, 2048], P('row', 'col'), may hold values from -0.125 to 0.125
- w_key: bfloat16 [2048, 256], P('row', 'col'), may hold values from -0.125 to 0.125
- w_value: bfloat16 [2048, 256], P('row', 'col'), may hold values from -0.125 to 0.125
- w_output: bfloat16 [2048, 2048], P('row', 'col'), may hold values from -0.5 to 0.5
- ffn_gain: float32 [2048], replicated, may hold values from 0.5 to 1.5
- w_gate: bfloat16 [2048, 5632], P('row', 'col'), may hold values from -0.125 to 0.125
- w_up: bfloat16 [2048, 5632], P('row', 'col'), may hold values from -0.125 to 0.125
- w_down: bfloat16 [2048, 5632], P('row', 'col'), may hold values from -0.078125 to 0.078125
Outputs:
- output: bfloat16 [16384, 2048], P('row', 'col')
- input_grad: bfloat16 [16384, 2048], P('row', 'col')
- attn_gain_grad: float32 [2048], P('row')
- w_query_grad: float32 [2048, 2048], P('row', 'col')
- w_key_grad: float32 [2048, 256], P('row', 'col')
- w_value_grad: float32 [2048, 256], P('row', 'col')
- w_output_grad: float32 [2048, 2048], P('row', 'col')
- ffn_gain_grad: float32 [2048], P('row')
- w_gate_grad: float32 [2048, 5632], P('row', 'col')
- w_up_grad: float32 [2048, 5632], P('row', 'col')
- w_down_grad: float32 [2048, 5632], P('row', 'col')
Inputs may be any that keep to these rules, and one draw needn't show every extreme that they name: `destination`: A permutation; the tokens of each aligned block of 512 arriving tokens go to exactly 16 places in each aligned block of 512 balanced places. `segment_ids`: within each aligned block of 512 places the ids start at 0 and rise by one where a new sequence begins, so a block holds at most 8 sequences; in every draw some block holds a single sequence of 512 tokens and some block holds 8 sequences.
All inputs are finite; a program needn't handle non-finite values.
Results may differ from a plain program's by a relative error of at most 0.028.
Values may be sent and summed in bfloat16 or wider, within the bound.
No kernel may reach another device: no remote copies, remote signals or barrier semaphores. Data moves between devices by JAX's collectives and lax.ppermute only.
A program may use at most 128 MiB of HBM per device.

v0:
```python
from functools import partial
import jax
import jax.numpy as jnp
from jax import lax
from jax.sharding import PartitionSpec as P

HEADS = 32
KV = 4
HD = 64
EPS = 1e-05
ROPE_BASE = 10000.0


def rope_tables(positions):
    half_width = HD // 2
    freqs = ROPE_BASE ** (-(jnp.arange(half_width, dtype=jnp.float32) * 2.0 / HD))
    angles = positions.astype(jnp.float32)[:, None] * freqs[None, :]
    return (jnp.cos(angles)[:, None, :], jnp.sin(angles)[:, None, :])


def rotate(values, cosine, sine):
    half_width = values.shape[-1] // 2
    first = values[..., :half_width]
    second = values[..., half_width:]
    return jnp.concatenate(
        [first * cosine - second * sine, second * cosine + first * sine], axis=-1
    )


def rotate_back(grads, cosine, sine):
    half_width = grads.shape[-1] // 2
    first = grads[..., :half_width]
    second = grads[..., half_width:]
    return jnp.concatenate(
        [first * cosine + second * sine, second * cosine - first * sine], axis=-1
    )


def positions_of(segment_ids):
    index = jnp.arange(segment_ids.shape[0], dtype=jnp.int32)
    change = jnp.concatenate([jnp.ones((1,), dtype=jnp.bool_), segment_ids[1:] != segment_ids[:-1]])
    starts = jnp.where(change, index, jnp.zeros_like(index))
    return index - lax.cummax(starts, axis=0)


def allowed_pairs(segment_ids):
    index = jnp.arange(segment_ids.shape[0], dtype=jnp.int32)
    return (segment_ids[:, None] == segment_ids[None, :]) & (index[None, :] <= index[:, None])


def rms_scale(values):
    return lax.rsqrt(jnp.mean(values * values, axis=-1, keepdims=True) + EPS)


def norm_back(values, inv_root, gain, grads):
    normed = values * inv_root
    scaled = grads * gain
    result = inv_root * (scaled - normed * jnp.mean(scaled * normed, axis=-1, keepdims=True))
    return (result, jnp.sum(grads * normed, axis=0))


def matmul(left, right):
    return jnp.dot(left, right, preferred_element_type=jnp.float32)


def head_scores(query_head, key_head, allowed, scale_factor):
    scores = matmul(query_head, key_head.T) * scale_factor
    return jnp.where(allowed, scores, -1e30)


def head_forward(inputs, key_heads, value_heads, allowed, scale_factor):
    query_head, kv_slot = inputs
    scores = head_scores(query_head, key_heads[kv_slot], allowed, scale_factor)
    peak = jnp.max(scores, axis=-1, keepdims=True)
    expo = jnp.exp(scores - peak)
    total = jnp.sum(expo, axis=-1, keepdims=True)
    probs = expo / total
    mixed = matmul(probs.astype(jnp.bfloat16), value_heads[kv_slot])
    return (mixed, (peak + jnp.log(total))[:, 0])


def head_backward(inputs, key_heads, value_heads, allowed, scale_factor):
    query_head, kv_slot, grad_head, log_total = inputs
    key_head = key_heads[kv_slot]
    value_head = value_heads[kv_slot]
    scores = head_scores(query_head, key_head, allowed, scale_factor)
    probs = jnp.exp(scores - log_total[:, None])
    prob_grad = matmul(grad_head, value_head.T)
    value_grad = matmul(probs.astype(jnp.bfloat16).T, grad_head)
    inner = jnp.sum(probs * prob_grad, axis=-1, keepdims=True)
    score_grad = (probs * (prob_grad - inner)).astype(jnp.bfloat16)
    query_grad = matmul(score_grad, key_head) * scale_factor
    key_grad = matmul(score_grad.T, query_head) * scale_factor
    return (query_grad, key_grad, value_grad)


def gather_rows(parts):
    widths = [part.shape[1] for part in parts]
    packed = lax.all_gather(jnp.concatenate(parts, axis=1), "row", axis=0, tiled=True)
    pieces = []
    offset = 0
    for width in widths:
        pieces.append(packed[:, offset : offset + width])
        offset += width
    return pieces


def scatter_rows(parts):
    columns = [part.reshape(part.shape[0], -1).astype(jnp.bfloat16) for part in parts]
    widths = [column.shape[1] for column in columns]
    packed = lax.psum_scatter(
        jnp.concatenate(columns, axis=1), "row", scatter_dimension=0, tiled=True
    ).astype(jnp.float32)
    pieces = []
    offset = 0
    for part, width in zip(parts, widths):
        piece = packed[:, offset : offset + width]
        pieces.append(piece.reshape(-1) if part.ndim == 1 else piece)
        offset += width
    return pieces


def body(
    tokens,
    cotangent,
    destination,
    segment_ids,
    attn_gain,
    w_query,
    w_key,
    w_value,
    w_output,
    ffn_gain,
    w_gate,
    w_up,
    w_down,
):
    row_count = tokens.shape[0]
    quarter = tokens.shape[1]
    col_start = lax.axis_index("col") * quarter
    group_size = HEADS // KV
    send_order = jnp.argsort(destination)
    slot_ids = destination[send_order] % row_count
    arrived_rows, arrived_grads, arrived_slots = (
        lax.all_to_all(tokens[send_order], "row", split_axis=0, concat_axis=0, tiled=True),
        lax.all_to_all(cotangent[send_order], "row", split_axis=0, concat_axis=0, tiled=True),
        lax.all_to_all(slot_ids, "row", split_axis=0, concat_axis=0, tiled=True),
    )
    placing = jnp.argsort(arrived_slots)
    full_rows, full_grads = (
        lax.all_gather(arrived_rows[placing], "col", axis=1, tiled=True),
        lax.all_gather(arrived_grads[placing], "col", axis=1, tiled=True),
    )
    query_w, key_w, value_w, output_w = gather_rows([w_query, w_key, w_value, w_output])
    cosine, sine = rope_tables(positions_of(segment_ids))
    allowed = allowed_pairs(segment_ids)
    rows_wide = full_rows.astype(jnp.float32)
    inv_one = rms_scale(rows_wide)
    normed_one = (rows_wide * inv_one * attn_gain).astype(jnp.bfloat16)
    query = matmul(normed_one, query_w)
    key_raw = matmul(normed_one, key_w)
    value_raw = matmul(normed_one, value_w)
    query_heads_count = query.shape[1] // HD
    kv_count = key_raw.shape[1] // HD
    query_rot = (
        rotate(query.reshape(row_count, query_heads_count, HD), cosine, sine)
        .astype(jnp.bfloat16)
        .transpose(1, 0, 2)
    )
    key_rot = (
        rotate(key_raw.reshape(row_count, kv_count, HD), cosine, sine)
        .astype(jnp.bfloat16)
        .transpose(1, 0, 2)
    )
    value_heads = value_raw.astype(jnp.bfloat16).reshape(row_count, kv_count, HD).transpose(1, 0, 2)
    kv_slots = jnp.arange(query_heads_count, dtype=jnp.int32) // group_size
    scale_factor = HD ** (-0.5)
    mixed_heads, log_totals = lax.map(
        partial(
            head_forward,
            key_heads=key_rot,
            value_heads=value_heads,
            allowed=allowed,
            scale_factor=scale_factor,
        ),
        (query_rot, kv_slots),
    )
    mixed = (
        mixed_heads.transpose(1, 0, 2)
        .reshape(row_count, query_heads_count * HD)
        .astype(jnp.bfloat16)
    )
    attn_terms = matmul(mixed, output_w.T)
    attn_full = lax.psum(attn_terms, "col")
    resid = rows_wide + attn_full
    inv_two = rms_scale(resid)
    normed_two = (resid * inv_two * ffn_gain).astype(jnp.bfloat16)
    resid_part = lax.dynamic_slice_in_dim(resid, col_start, quarter, 1)
    gate_w, up_w, down_w = gather_rows([w_gate, w_up, w_down])
    gate = matmul(normed_two, gate_w)
    upper = matmul(normed_two, up_w)
    sigmoid_gate = jax.nn.sigmoid(gate)
    activ = (gate * sigmoid_gate * upper).astype(jnp.bfloat16)
    ffn_share = lax.psum_scatter(
        matmul(activ, down_w.T).astype(jnp.bfloat16), "col", scatter_dimension=1, tiled=True
    ).astype(jnp.float32)
    output_share = (resid_part + ffn_share).astype(jnp.bfloat16)
    down_weight_grad = matmul(full_grads.T, activ)
    act_grad = matmul(full_grads, down_w)
    gate_grad = (act_grad * upper * sigmoid_gate * (1.0 + gate * (1.0 - sigmoid_gate))).astype(
        jnp.bfloat16
    )
    up_grad = (act_grad * gate * sigmoid_gate).astype(jnp.bfloat16)
    gate_weight_grad = matmul(normed_two.T, gate_grad)
    up_weight_grad = matmul(normed_two.T, up_grad)
    normed_terms_two = matmul(gate_grad, gate_w.T) + matmul(up_grad, up_w.T)
    normed_grad_two = lax.psum(normed_terms_two, "col")
    resid_norm_grad, ffn_gain_grad = norm_back(resid, inv_two, ffn_gain, normed_grad_two)
    resid_grad = full_grads.astype(jnp.float32) + resid_norm_grad
    attn_grad_low = resid_grad.astype(jnp.bfloat16)
    output_weight_grad = matmul(attn_grad_low.T, mixed)
    mixed_grad = matmul(attn_grad_low, output_w).astype(jnp.bfloat16)
    mixed_grad_heads = mixed_grad.reshape(row_count, query_heads_count, HD).transpose(1, 0, 2)
    query_grads, key_grads, value_grads = lax.map(
        partial(
            head_backward,
            key_heads=key_rot,
            value_heads=value_heads,
            allowed=allowed,
            scale_factor=scale_factor,
        ),
        (query_rot, kv_slots, mixed_grad_heads, log_totals),
    )
    query_grad = (
        rotate_back(query_grads.transpose(1, 0, 2), cosine, sine)
        .reshape(row_count, query_heads_count * HD)
        .astype(jnp.bfloat16)
    )
    key_sum = key_grads.reshape(kv_count, group_size, row_count, HD).sum(axis=1).transpose(1, 0, 2)
    key_grad = (
        rotate_back(key_sum, cosine, sine).reshape(row_count, kv_count * HD).astype(jnp.bfloat16)
    )
    value_sum = (
        value_grads.reshape(kv_count, group_size, row_count, HD).sum(axis=1).transpose(1, 0, 2)
    )
    value_grad = value_sum.reshape(row_count, kv_count * HD).astype(jnp.bfloat16)
    query_weight_grad = matmul(normed_one.T, query_grad)
    key_weight_grad = matmul(normed_one.T, key_grad)
    value_weight_grad = matmul(normed_one.T, value_grad)
    normed_terms_one = (
        matmul(query_grad, query_w.T) + matmul(key_grad, key_w.T) + matmul(value_grad, value_w.T)
    )
    normed_grad_one = lax.psum(normed_terms_one.astype(jnp.bfloat16), "col").astype(jnp.float32)
    rows_norm_grad, attn_gain_grad = norm_back(rows_wide, inv_one, attn_gain, normed_grad_one)
    rows_grad = resid_grad + rows_norm_grad
    input_share = lax.dynamic_slice_in_dim(rows_grad, col_start, quarter, 1).astype(jnp.bfloat16)
    (
        query_result,
        key_result,
        value_result,
        output_result,
        gate_result,
        up_result,
        down_result,
        attn_gain_result,
        ffn_gain_result,
    ) = scatter_rows(
        [
            query_weight_grad,
            key_weight_grad,
            value_weight_grad,
            output_weight_grad,
            gate_weight_grad,
            up_weight_grad,
            down_weight_grad,
            attn_gain_grad,
            ffn_gain_grad,
        ]
    )
    back_rows, back_grads = (
        lax.all_to_all(output_share[arrived_slots], "row", split_axis=0, concat_axis=0, tiled=True),
        lax.all_to_all(input_share[arrived_slots], "row", split_axis=0, concat_axis=0, tiled=True),
    )
    restore = jnp.argsort(send_order)
    return (
        back_rows[restore],
        back_grads[restore],
        attn_gain_result,
        query_result,
        key_result,
        value_result,
        output_result,
        ffn_gain_result,
        gate_result,
        up_result,
        down_result,
    )


def solution(mesh):
    placed = (
        P("row", "col"),
        P("row", "col"),
        P("row"),
        P("row"),
        P(),
        P("row", "col"),
        P("row", "col"),
        P("row", "col"),
        P("row", "col"),
        P(),
        P("row", "col"),
        P("row", "col"),
        P("row", "col"),
    )
    return jax.shard_map(
        body,
        mesh=mesh,
        in_specs=placed,
        out_specs=(
            P("row", "col"),
            P("row", "col"),
            P("row"),
            P("row", "col"),
            P("row", "col"),
            P("row", "col"),
            P("row", "col"),
            P("row"),
            P("row", "col"),
            P("row", "col"),
            P("row", "col"),
        ),
        check_vma=False,
    )
```

profile of v0, /device:TPU:1, one launch (start us, length us, event | category | flops | bytes accessed | tf_op | source)
XLA Modules:
  0.0 914.6 jit_solution(13303859457156370730)
XLA Ops:
  7.2 4.5 sort.45
  12.3 3.6 gather_fusion.1
  16.6 9.6 %all-to-all-start.1 = ((s32[32,16,1]{1,2,0:T(1,128)}), s32[32,16,1]{1,2,0:T(1,128)S(1)}, u32[]{:S(2)}, u32[]{:S(2)}) async-start(s32[32,16,1]{1,2,0:T(1,128)} %bitcast.2), calls=%async_computation.1 | async-start | bytes 32768 | tf_op jit(solution)/shard_map/all_to_all | solution.py:147
  26.2 2.6 gather_fusion
  28.9 4.2 all-to-all-done.1
  33.1 4.2 all-to-all-start
  38.6 3.8 sort.46
  42.4 6.5 all-to-all-done
  48.9 2.6 gather_fusion.2
  53.7 26.4 %all-gather.11.cloned.1.call-done = bf16[512,2048]{1,0:T(8,128)(2,1)} async-done(((bf16[512,512]{1,0:T(8,128)(2,1)}), bf16[512,2048]{1,0:T(8,128)(2,1)}) %all-gather.11.cloned.1.call-update) | async-done | bytes 2097168 | tf_op jit(solution)/shard_map/all_gather | solution.py:151
  80.0 2.1 fusion.54
  82.1 48.2 %all-gather.7.cloned.1.call-done = bf16[2048,1152]{1,0:T(8,128)(2,1)} async-done(((bf16[64,1152]{1,0:T(8,128)(2,1)}), bf16[2048,1152]{1,0:T(8,128)(2,1)}) %all-gather.7.cloned.1.call-update) | async-done | bytes 4718608 | tf_op jit(solution)/shard_map/all_gather | solution.py:99
  130.3 3.6 fusion.67
  135.6 1.9 convolution_bitcast_fusion.2
  138.0 2.0 fusion.72
  140.1 25.1 %while.32 = (s32[]{:T(128)}, bf16[8,512,64]{1,2,0:T(8,128)(2,1)S(1)}, f32[8,512]{1,0:T(8,128)}, bf16[8,512,64]{2,1,0:T(8,128)(2,1)}, bf16[1,512,64]{2,1,0:T(8,12...) while((s32[]{:T(128)}, bf16[8,512,64]{1,2,0:T(8,128)(2,1)S(1)}, ...), condition=%wide.region_8.9_spmd.clone.clone, body=%wide.region_5.8_spmd.clone.sunk.clone | while | flops 69991936 | bytes 3694689 | solution.py:178
  166.0 5.0 fusion.63
  172.0 2.0 gather_fusion.5
  174.0 16.6 %all_to_all.60 = bf16[32,16,512]{2,1,0:T(8,128)(2,1)S(1)} all-to-all(bf16[32,16,512]{2,1,0:T(8,128)(2,1)S(1)} %bitcast.184), channel_id=1, replica_groups=mesh['row'=32,'col'=4] {'row'}, dimensions={0} | all-to-all | bytes 1048576 | tf_op jit(solution)/shard_map/all_to_all | solution.py:146
  190.6 2.6 gather_fusion.6
  195.2 67.6 %all-reduce.4.cloned.1.call-done = f32[512,2048]{1,0:T(8,128)} async-done(((f32[512,2048]{1,0:T(8,128)}), f32[512,2048]{1,0:T(8,128)}) %all-reduce.4.cloned.1.call-update) | async-done | bytes 4194320 | tf_op jit(solution)/shard_map/psum | solution.py:194
  262.7 2.8 multiply_reduce_fusion.4
  265.6 2.0 copy-done.2
  269.3 26.3 %all-gather.13.cloned.1.call-done = bf16[512,2048]{1,0:T(8,128)(2,1)} async-done(((bf16[512,512]{1,0:T(8,128)(2,1)}), bf16[512,2048]{1,0:T(8,128)(2,1)}) %all-gather.13.cloned.1.call-update) | async-done | bytes 2097168 | tf_op jit(solution)/shard_map/all_gather | solution.py:152
  295.7 76.7 %all-gather.9.cloned.1.call-done = bf16[2048,4224]{1,0:T(8,128)(2,1)} async-done(((bf16[64,4224]{1,0:T(8,128)(2,1)}), bf16[2048,4224]{1,0:T(8,128)(2,1)}) %all-gather.9.cloned.1.call-update) | async-done | bytes 17301520 | tf_op jit(solution)/shard_map/all_gather | solution.py:99
  372.4 6.5 fusion.41
  378.9 2.3 copy-done.31
  381.3 5.0 fusion.47
  386.2 7.3 multiply_convert_fusion.4
  393.6 5.4 fusion.45
  398.9 5.0 fusion.55
  404.0 9.7 %all-reduce.8.cloned.1.call-start = ((), (), s32[]{:S(2)}) async-start(), calls=%async_computation.12 | async-start | bytes 4194304 | tf_op jit(solution)/shard_map/psum | solution.py:253
  413.7 82.1 %all-reduce.6.cloned.1.call-done = f32[512,2048]{1,0:T(8,128)} async-done(((f32[512,2048]{1,0:T(8,128)}), f32[512,2048]{1,0:T(8,128)}) %all-reduce.6.cloned.1.call-update) | async-done | bytes 4194320 | tf_op jit(solution)/shard_map/psum | solution.py:217
  495.9 4.6 multiply_reduce_fusion.1
  501.8 2.7 multiply_add_fusion
  504.5 1.9 copy-done.7
  506.4 3.7 fusion.69
  511.6 50.9 %while.33 = (s32[]{:T(128)}, f32[8,512,64]{1,2,0:T(8,128)}, f32[8,512,64]{1,2,0:T(8,128)}, f32[8,512,64]{1,2,0:T(8,128)}, bf16[8,512,64]{2,1,0:T(8,128)(2,1)}, /...) while((s32[]{:T(128)}, f32[8,512,64]{1,2,0:T(8,128)}, ...), condition=%wide.region_17.18_spmd.clone.clone, body=%wide.region_15.17_spmd.clone.sunk.clone | while | flops 170982912 | bytes 9126013 | solution.py:224
  540.6 1.9 fusion.176
  567.5 2.9 fusion.65
  572.2 3.2 add_convert_fusion
  575.5 7.9 fusion.58
  583.5 7.9 convolution_convert_fusion.2
  591.4 5.3 convolution_convert_fusion.1
  596.7 5.0 convolution_convert_fusion
  603.4 2.7 convolution_convert_fusion.4
  606.1 2.6 convolution_convert_fusion.3
  608.7 25.4 %all-reduce.8.cloned.1.call-done = bf16[512,2048]{1,0:T(8,128)(2,1)} async-done(((bf16[512,2048]{1,0:T(8,128)(2,1)}), bf16[512,2048]{1,0:T(8,128)(2,1)}) %all-reduce.8.cloned.1.call-update) | async-done | bytes 2097168 | tf_op jit(solution)/shard_map/psum | solution.py:253
  634.1 6.1 fusion.53
  640.2 93.2 %concatenate.53 = bf16[2048,5378]{0,1:T(8,128)(2,1)} concatenate(bf16[2048,512]{0,1:T(8,128)(2,1)} %convolution_convert_fusion.4, bf16[2048,64]{0,1:T(8,128)(2,1)S(1)} %convolution_convert_fusion.6, bf16[2048,64]{0,1:T(8,128)(2,1)S(1)} %convolution_convert_fusion.5, bf16[2048,512]{0,1:T(8,128)(2,1)} %convolution_convert_fusion.3, bf16[2048,1408]{0,1:T(8,128)(2,1)} %convolution_convert_fusion.2, ...), dimensions={1} | concatenate | bytes 44056576 | tf_op jit(solution)/shard_map/concatenate | solution.py:112
  733.5 28.4 %copy.67 = bf16[2048,5378]{1,0:T(8,128)(2,1)} copy(bf16[2048,5378]{0,1:T(8,128)(2,1)} %concatenate.53) | data formatting | bytes 44056576
  764.3 2.6 gather_fusion.3
  766.9 7.7 all-to-all-start.2
  774.6 2.5 fusion.73
  777.1 2.6 gather_fusion.7
  779.8 6.4 all-to-all-done.2
  786.1 4.4 all-to-all-start.4
  790.5 3.8 sort.47
  794.3 2.6 gather_fusion.4
  796.9 5.1 all-to-all-done.4
  802.1 2.6 gather_fusion.8
  804.7 89.5 %reduce-scatter.7.cloned.1.call-done = bf16[64,5378]{1,0:T(8,128)(2,1)} async-done(((bf16[2048,5378]{1,0:T(8,128)(2,1)}), bf16[64,5378]{1,0:T(8,128)(2,1)}) %reduce-scatter.7.cloned.1.call-update) | async-done | bytes 688400
  894.2 2.0 copy.68
  903.6 2.1 copy.64
  (248 shorter events, 109.3 us)
Async XLA Ops:
  7.2 19.0 %copy-start = (bf16[512,512]{1,0:T(8,128)(2,1)S(1)}, bf16[512,512]{1,0:T(8,128)(2,1)}, u32[]{:S(2)}) copy-start(bf16[512,512]{1,0:T(8,128)(2,1)} %param.17) | copy-start | bytes 1572868
  11.7 0.6 copy-start.28
  16.6 16.5 %all-to-all-start.1 = ((s32[32,16,1]{1,2,0:T(1,128)}), s32[32,16,1]{1,2,0:T(1,128)S(1)}, u32[]{:S(2)}, u32[]{:S(2)}) async-start(s32[32,16,1]{1,2,0:T(1,128)} %bitcast.2), calls=%async_computation.1 | async-start | bytes 32768 | tf_op jit(solution)/shard_map/all_to_all | solution.py:147
  28.9 22.8 %copy-start.19 = (bf16[64,512]{1,0:T(8,128)(2,1)S(1)}, bf16[64,512]{1,0:T(8,128)(2,1)}, u32[]{:S(2)}) copy-start(bf16[64,512]{1,0:T(8,128)(2,1)} %param.22) | copy-start | bytes 196612
  28.9 22.8 %copy-start.20 = (bf16[64,512]{1,0:T(8,128)(2,1)S(1)}, bf16[64,512]{1,0:T(8,128)(2,1)}, u32[]{:S(2)}) copy-start(bf16[64,512]{1,0:T(8,128)(2,1)} %param.25) | copy-start | bytes 196612
  28.9 22.8 %copy-start.21 = (bf16[64,64]{1,0:T(8,128)(2,1)S(1)}, bf16[64,64]{1,0:T(8,128)(2,1)}, u32[]{:S(2)}) copy-start(bf16[64,64]{1,0:T(8,128)(2,1)} %param.23) | copy-start | bytes 24580
  28.9 22.8 %copy-start.22 = (bf16[64,64]{1,0:T(8,128)(2,1)S(1)}, bf16[64,64]{1,0:T(8,128)(2,1)}, u32[]{:S(2)}) copy-start(bf16[64,64]{1,0:T(8,128)(2,1)} %param.24) | copy-start | bytes 24580
  28.9 23.7 %copy-start.25 = (s32[512]{0:T(512)S(1)}, s32[512]{0:T(512)}, u32[]{:S(2)}) copy-start(s32[512]{0:T(512)} %param.20) | copy-start | bytes 6148
  33.1 49.0 %copy-start.16 = (s32[32,16,1]{1,2,0:T(1,128)}, s32[32,16,1]{1,2,0:T(1,128)S(1)}, u32[]{:S(2)}) copy-start(s32[32,16,1]{1,2,0:T(1,128)S(1)} %all-to-all-done.1) | copy-start | bytes 6148
  33.1 15.9 %all-to-all-start = ((bf16[32,16,512]{2,1,0:T(8,128)(2,1)}), bf16[32,16,512]{2,1,0:T(8,128)(2,1)S(1)}, u32[]{:S(2)}, u32[]{:S(2)}) async-start(bf16[32,16,512]{2,1,0:T(8,128)(2,1)} %bitcast), calls=%async_computation | async-start | bytes 1048576 | tf_op jit(solution)/shard_map/all_to_all | solution.py:145
  37.3 42.7 %all-gather.11.cloned.1.call-start = ((), (), s32[]{:S(2)}) async-start(), calls=%async_computation.13 | async-start | bytes 2621440 | tf_op jit(solution)/shard_map/all_gather | solution.py:151
  48.9 81.4 %copy-start.23 = (f32[2048]{0:T(1024)S(1)}, f32[2048]{0:T(1024)}, u32[]{:S(2)}) copy-start(f32[2048]{0:T(1024)} %param.21) | copy-start | bytes 24580
  51.6 78.8 %all-gather.7.cloned.1.call-start = ((), (), s32[]{:S(2)}) async-start(), calls=%async_computation.7 | async-start | bytes 4866048 | tf_op jit(solution)/shard_map/all_gather | solution.py:99
  52.5 210.3 %all-reduce.4.cloned.1.call-start = ((), (), s32[]{:S(2)}) async-start(), calls=%async_computation.8 | async-start | bytes 8388608 | tf_op jit(solution)/shard_map/psum | solution.py:194
  53.1 84.4 %copy-start.30 = (f32[32]{0:T(128)}, f32[32]{0:T(128)S(1)}, u32[]{:S(2)}) copy-start(f32[32]{0:T(128)S(1)} %negate_power_fusion) | copy-start | bytes 388
  134.0 1.7 copy-start.5
  135.6 4.5 copy-start.26
  165.2 0.8 copy-start.9
  171.0 1.0 copy-start.4
  171.0 124.6 %all-gather.13.cloned.1.call-start = ((), (), s32[]{:S(2)}) async-start(), calls=%async_computation.14 | async-start | bytes 2621440 | tf_op jit(solution)/shard_map/all_gather | solution.py:152
  190.6 2.7 copy-start.14
  190.6 2.7 copy-start.15
  193.3 179.1 %all-gather.9.cloned.1.call-start = ((), (), s32[]{:S(2)}) async-start(), calls=%async_computation.9 | async-start | bytes 17842176 | tf_op jit(solution)/shard_map/all_gather | solution.py:99
  195.1 72.5 %copy-start.18 = (f32[2048]{0:T(1024)S(1)}, f32[2048]{0:T(1024)}, u32[]{:S(2)}) copy-start(f32[2048]{0:T(1024)} %param.26) | copy-start | bytes 24580
  195.1 300.7 %all-reduce.6.cloned.1.call-start = ((), (), s32[]{:S(2)}) async-start(), calls=%async_computation.11 | async-start | bytes 8388608 | tf_op jit(solution)/shard_map/psum | solution.py:217
  265.6 2.1 copy-start.2
  372.4 6.6 copy-start.11
  372.4 8.9 copy-start.31
  393.6 5.4 copy-start.32
  404.0 230.1 %all-reduce.8.cloned.1.call-start = ((), (), s32[]{:S(2)}) async-start(), calls=%async_computation.12 | async-start | bytes 4194304 | tf_op jit(solution)/shard_map/psum | solution.py:253
  495.9 4.6 copy-start.3
  495.9 5.9 copy-start.6
  504.4 1.9 copy-start.7
  506.4 5.2 copy-start.27
  575.4 187.3 %reduce-scatter.5.cloned.1.call-start = ((), (), s32[]{:S(2)}) async-start(), calls=%async_computation.10 | async-start | bytes 2621440 | tf_op jit(solution)/shard_map/reduce_scatter | solution.py:204
  583.4 310.8 %reduce-scatter.7.cloned.1.call-start = ((), (), s32[]{:S(2)}) async-start(), calls=%async_computation.15 | async-start | bytes 23248896
  583.4 8.0 copy-start.12
  583.5 7.9 copy-start.34
  591.4 5.3 copy-start.13
  591.4 5.3 copy-start.33
  596.7 5.0 copy-start.24
  603.3 2.8 copy-start.8
  603.3 2.7 copy-start.10
  761.9 0.7 copy-start.17
  766.9 19.3 %all-to-all-start.2 = ((bf16[32,16,512]{2,1,0:T(8,128)(2,1)}), bf16[32,16,512]{2,1,0:T(8,128)(2,1)S(1)}, u32[]{:S(2)}, u32[]{:S(2)}) async-start(bf16[32,16,512]{2,1,0:T(8,128)(2,1)} %bitcast.14), calls=%async_computation.3 | async-start | bytes 1048576 | tf_op jit(solution)/shard_map/all_to_all | solution.py:281
  774.6 15.9 %copy-start.29 = (s32[512]{0:T(512)S(1)}, s32[512]{0:T(512)}, u32[]{:S(2)}) copy-start(s32[512]{0:T(512)} %copy-done.28) | copy-start | bytes 6148
  786.1 15.9 %all-to-all-start.4 = ((bf16[32,16,512]{2,1,0:T(8,128)(2,1)}), bf16[32,16,512]{2,1,0:T(8,128)(2,1)S(1)}, u32[]{:S(2)}, u32[]{:S(2)}) async-start(bf16[32,16,512]{2,1,0:T(8,128)(2,1)} %bitcast.24), calls=%async_computation.5 | async-start | bytes 1048576 | tf_op jit(solution)/shard_map/all_to_all | solution.py:282
  897.2 10.4 %copy-start.1 = (bf16[512,512]{1,0:T(8,128)(2,1)S(1)}, bf16[512,512]{1,0:T(8,128)(2,1)}, u32[]{:S(2)}) copy-start(bf16[512,512]{1,0:T(8,128)(2,1)} %param.17) | copy-start | bytes 1572868
Sparse Core Ops, SparseCore 0:
  51.7 28.2 all-gather.10
  82.8 47.4 all-gather.6
  171.1 91.5 all-reduce.3
  264.9 30.6 all-gather.12
  298.0 74.3 all-gather.8
  404.1 91.7 all-reduce.5
  575.6 58.4 all-reduce.7
  636.6 29.4 reduce-scatter.4
  762.0 132.1 reduce-scatter.6
where the time goes:
time: 928 us; the launch traced here: 915 us
  waiting for transfers between devices  465 us (50%)
  local copies, waits for them, and re-layouts  191 us (21%)
  matrix products  142 us (15%)
  other arithmetic  49.6 us (5%)
  starting transfers between devices  36.1 us (4%)
  blocking collectives  16.6 us (2%)
  between operations  14.9 us (2%)
    dot_general x77, matrix products, matmul(): return jnp.dot(left, right, preferred_element_type=jnp.float32)  142 us
    all_gather x2, waiting for transfers between devices, gather_rows(): lax.all_gather(jnp.concatenate(parts, axis=1), 'row', axis=0, tiled=True)  125 us
    concatenate x1, local copies, waits for them, and re-layouts, scatter_rows(): jnp.concatenate(columns, axis=1)  93.2 us
    unnamed x10, waiting for transfers between devices  89.6 us
    psum x1, waiting for transfers between devices, body(): normed_grad_two = lax.psum(normed_terms_two, 'col')  82.1 us
    psum x1, waiting for transfers between devices, body(): attn_full = lax.psum(attn_terms, 'col')  67.6 us
    unnamed x82, local copies, waits for them, and re-layouts  51.5 us
    all_gather x1, waiting for transfers between devices, body(): lax.all_gather(arrived_rows[placing], 'col', axis=1, tiled=True)  26.4 us
  transfers between devices with their start and end apart: 13, of which 12 were waited for; matrix products, arithmetic and copies ran while one was open for 22% of the time, Pallas kernels for 0%

commit v1 on v0

--- a/solution.py
+++ b/solution.py
@@ -9,6 +9,14 @@
 HD = 64
 EPS = 1e-05
 ROPE_BASE = 10000.0
+
+
+def add_in_pairs(block, axis):
+    count, acc = (lax.axis_size(axis), block)
+    for far in [1 << k for k in range(count.bit_length() - 1)]:
+        swap = [(i, i ^ far) for i in range(count)]
+        acc = acc + lax.ppermute(acc, axis, swap)
+    return acc
 
 
 def rope_tables(positions):
@@ -191,7 +199,7 @@
         .astype(jnp.bfloat16)
     )
     attn_terms = matmul(mixed, output_w.T)
-    attn_full = lax.psum(attn_terms, "col")
+    attn_full = add_in_pairs(attn_terms, "col")
     resid = rows_wide + attn_full
     inv_two = rms_scale(resid)
     normed_two = (resid * inv_two * ffn_gain).astype(jnp.bfloat16)

time: 928 us -> 928 us (level)
  matrix products: 142 us -> 154 us
    ppermute x0 -> x2, waiting for transfers between devices: none -> 181 us  [add_in_pairs(): acc = acc + lax.ppermute(acc, axis, swap)]
    all_gather x2, waiting for transfers between devices: 125 us -> 48.2 us  [gather_rows(): lax.all_gather(jnp.concatenate(parts, axis=1), 'row', axis=0, tiled=True)]
    psum x1 -> x0, waiting for transfers between devices: 67.6 us -> none  [body(): attn_full = lax.psum(attn_terms, 'col')]
    all_gather x1, waiting for transfers between devices: 26.3 us -> 0.01 us  [body(): lax.all_gather(arrived_grads[placing], 'col', axis=1, tiled=True)]
    all_gather x1, waiting for transfers between devices: 26.4 us -> 5.15 us  [body(): lax.all_gather(arrived_rows[placing], 'col', axis=1, tiled=True)]
    dot_general x77, matrix products: 142 us -> 154 us  [matmul(): return jnp.dot(left, right, preferred_element_type=jnp.float32)]
    psum x1, waiting for transfers between devices: 82.1 us -> 92.9 us  [body(): normed_grad_two = lax.psum(normed_terms_two, 'col')]
    unnamed x82 -> x84, local copies, waits for them, and re-layouts: 51.5 us -> 49 us
  transfers between devices with their start and end apart: 13 -> 14, of which waited for: 12 -> 11; matrix products, arithmetic and copies ran while one was open for 22% -> 26% of each run, Pallas kernels for 0% -> 0%
where the time goes in v1:
time: 928 us; the launch traced here: 917 us
  waiting for transfers between devices  463 us (50%)
  local copies, waits for them, and re-layouts  189 us (20%)
  matrix products  154 us (17%)
  other arithmetic  49.4 us (5%)
  starting transfers between devices  30.9 us (3%)
  blocking collectives  15.4 us (2%)
  between operations  15 us (2%)
    ppermute x2, waiting for transfers between devices, add_in_pairs(): acc = acc + lax.ppermute(acc, axis, swap)  181 us
    dot_general x77, matrix products, matmul(): return jnp.dot(left, right, preferred_element_type=jnp.float32)  154 us
    concatenate x1, local copies, waits for them, and re-layouts, scatter_rows(): jnp.concatenate(columns, axis=1)  93.5 us
    psum x1, waiting for transfers between devices, body(): normed_grad_two = lax.psum(normed_terms_two, 'col')  92.9 us
    unnamed x9, waiting for transfers between devices  89.5 us
    unnamed x84, local copies, waits for them, and re-layouts  49 us
    all_gather x2, waiting for transfers between devices, gather_rows(): lax.all_gather(jnp.concatenate(parts, axis=1), 'row', axis=0, tiled=True)  48.2 us
    psum x1, waiting for transfers between devices, body(): lax.psum(normed_terms_one.astype(jnp.bfloat16), 'col').astype(jnp.float32)  24.7 us
  transfers between devices with their start and end apart: 14, of which 11 were waited for; matrix products, arithmetic and copies ran while one was open for 26% of the time, Pallas kernels for 0%

profile of v1, /device:TPU:1, one launch (start us, length us, event | category | flops | bytes accessed | tf_op | source)
XLA Modules:
  0.0 917.1 jit_solution(2304889747308429456)
XLA Ops:
  7.2 4.5 sort.45
  12.3 3.6 gather_fusion.1
  16.6 9.6 %all-to-all-start.1 = ((s32[32,16,1]{1,2,0:T(1,128)}), s32[32,16,1]{1,2,0:T(1,128)S(1)}, u32[]{:S(2)}, u32[]{:S(2)}) async-start(s32[32,16,1]{1,2,0:T(1,128)} %bitcast.2), calls=%async_computation.1 | async-start | bytes 32768 | tf_op jit(solution)/shard_map/all_to_all | solution.py:155
  26.2 2.6 gather_fusion
  28.9 4.2 all-to-all-done.1
  33.1 4.2 all-to-all-start
  38.6 3.8 sort.46
  42.4 6.5 all-to-all-done
  48.9 2.6 gather_fusion.2
  52.5 2.0 gather_fusion.5
  54.6 15.4 %all_to_all.60 = bf16[32,16,512]{2,1,0:T(8,128)(2,1)S(1)} all-to-all(bf16[32,16,512]{2,1,0:T(8,128)(2,1)S(1)} %bitcast.184), channel_id=1, replica_groups=mesh['row'=32,'col'=4] {'row'}, dimensions={0} | all-to-all | bytes 1048576 | tf_op jit(solution)/shard_map/all_to_all | solution.py:154
  69.9 2.6 gather_fusion.6
  74.9 5.1 all-gather.11.cloned.1.call-done
  80.0 2.1 fusion.54
  82.1 48.2 %all-gather.7.cloned.1.call-done = bf16[2048,1152]{1,0:T(8,128)(2,1)} async-done(((bf16[64,1152]{1,0:T(8,128)(2,1)}), bf16[2048,1152]{1,0:T(8,128)(2,1)}) %all-gather.7.cloned.1.call-update) | async-done | bytes 4718608 | tf_op jit(solution)/shard_map/all_gather | solution.py:107
  130.3 3.6 fusion.67
  135.6 1.9 convolution_bitcast_fusion.2
  138.0 2.0 fusion.72
  140.2 25.1 %while.32 = (s32[]{:T(128)}, bf16[8,512,64]{1,2,0:T(8,128)(2,1)S(1)}, f32[8,512]{1,0:T(8,128)}, bf16[8,512,64]{2,1,0:T(8,128)(2,1)}, bf16[1,512,64]{2,1,0:T(8,12...) while((s32[]{:T(128)}, bf16[8,512,64]{1,2,0:T(8,128)(2,1)S(1)}, ...), condition=%wide.region_8.9_spmd.clone.clone, body=%wide.region_5.8_spmd.clone.sunk.clone | while | flops 69991936 | bytes 3694689 | solution.py:186
  165.3 2.9 fusion.63
  169.4 90.8 %collective-permute-done = f32[512,2048]{1,0:T(8,128)S(1)} collective-permute-done((f32[512,2048]{1,0:T(8,128)S(1)}, f32[512,2048]{1,0:T(8,128)S(1)}, u32[]{:S(2)}, u32[]{:S(2)}) %collective-permute-start) | collective-permute-done | bytes 4194336 | tf_op jit(solution)/shard_map/ppermute | solution.py:18
  261.0 3.0 collective-permute-start.1
  263.9 89.9 %collective-permute-done.1 = f32[512,2048]{1,0:T(8,128)S(1)} collective-permute-done((f32[512,2048]{1,0:T(8,128)S(1)}, f32[512,2048]{1,0:T(8,128)S(1)}, u32[]{:S(2)}, u32[]{:S(2)}) %collective-permute-start.1) | collective-permute-done | bytes 4194336 | tf_op jit(solution)/shard_map/ppermute | solution.py:18
  355.0 2.1 copy-done.2
  358.7 6.6 fusion.41
  365.3 2.3 copy-done.32
  367.6 5.0 fusion.47
  372.6 7.3 multiply_convert_fusion.4
  380.0 5.4 fusion.45
  385.3 5.1 fusion.55
  390.9 92.9 %all-reduce.3.cloned.1.call-done = f32[512,2048]{1,0:T(8,128)} async-done(((f32[512,2048]{1,0:T(8,128)}), f32[512,2048]{1,0:T(8,128)}) %all-reduce.3.cloned.1.call-update) | async-done | bytes 4194320 | tf_op jit(solution)/shard_map/psum | solution.py:225
  483.9 4.6 multiply_reduce_fusion.1
  489.8 2.7 multiply_add_fusion
  492.5 1.9 copy-done.7
  494.4 2.9 fusion.69
  498.7 65.3 %while.33 = (s32[]{:T(128)}, f32[8,512,64]{1,2,0:T(8,128)}, f32[8,512,64]{1,2,0:T(8,128)}, f32[8,512,64]{1,2,0:T(8,128)}, bf16[8,512,64]{2,1,0:T(8,128)(2,1)}, /...) while((s32[]{:T(128)}, f32[8,512,64]{1,2,0:T(8,128)}, ...), condition=%wide.region_16.17_spmd.clone.clone, body=%wide.region_14.16_spmd.clone.sunk.clone | while | flops 170982912 | bytes 9060477 | solution.py:232
  545.8 1.9 fusion.177
  552.1 1.9 fusion.176
  564.0 2.1 add_convert_fusion.2
  570.7 2.9 fusion.65
  575.4 3.2 add_convert_fusion
  578.6 7.9 fusion.58
  586.6 7.9 convolution_convert_fusion.2
  594.6 5.2 convolution_convert_fusion.1
  599.8 5.1 convolution_convert_fusion
  607.2 2.8 convolution_convert_fusion.4
  609.9 2.6 convolution_convert_fusion.3
  612.6 24.7 %all-reduce.5.cloned.1.call-done = bf16[512,2048]{1,0:T(8,128)(2,1)} async-done(((bf16[512,2048]{1,0:T(8,128)(2,1)}), bf16[512,2048]{1,0:T(8,128)(2,1)}) %all-reduce.5.cloned.1.call-update) | async-done | bytes 2097168 | tf_op jit(solution)/shard_map/psum | solution.py:261
  637.3 6.2 fusion.53
  643.5 93.5 %concatenate.53 = bf16[2048,5378]{0,1:T(8,128)(2,1)} concatenate(bf16[2048,512]{0,1:T(8,128)(2,1)} %convolution_convert_fusion.4, bf16[2048,64]{0,1:T(8,128)(2,1)S(1)} %convolution_convert_fusion.6, bf16[2048,64]{0,1:T(8,128)(2,1)S(1)} %copy-done.12, bf16[2048,512]{0,1:T(8,128)(2,1)} %convolution_convert_fusion.3, bf16[2048,1408]{0,1:T(8,128)(2,1)} %convolution_convert_fusion.2, ...), dimensions={1} | concatenate | bytes 44056576 | tf_op jit(solution)/shard_map/concatenate | solution.py:120
  737.0 27.4 %copy.67 = bf16[2048,5378]{1,0:T(8,128)(2,1)} copy(bf16[2048,5378]{0,1:T(8,128)(2,1)} %concatenate.53) | data formatting | bytes 44056576
  766.8 2.6 gather_fusion.3
  769.4 7.7 all-to-all-start.2
  777.2 2.5 fusion.73
  779.7 2.6 gather_fusion.7
  782.3 6.4 all-to-all-done.2
  788.7 4.3 all-to-all-start.4
  793.0 3.8 sort.47
  796.8 2.6 gather_fusion.4
  799.4 5.1 all-to-all-done.4
  804.6 2.6 gather_fusion.8
  807.2 89.4 %reduce-scatter.7.cloned.1.call-done = bf16[64,5378]{1,0:T(8,128)(2,1)} async-done(((bf16[2048,5378]{1,0:T(8,128)(2,1)}), bf16[64,5378]{1,0:T(8,128)(2,1)}) %reduce-scatter.7.cloned.1.call-update) | async-done | bytes 688400
  896.6 2.0 copy.68
  906.0 2.1 copy.64
  (252 shorter events, 123.1 us)
Async XLA Ops:
  7.2 19.0 %copy-start = (bf16[512,512]{1,0:T(8,128)(2,1)S(1)}, bf16[512,512]{1,0:T(8,128)(2,1)}, u32[]{:S(2)}) copy-start(bf16[512,512]{1,0:T(8,128)(2,1)} %param.17) | copy-start | bytes 1572868
  11.7 0.6 copy-start.28
  16.6 16.5 %all-to-all-start.1 = ((s32[32,16,1]{1,2,0:T(1,128)}), s32[32,16,1]{1,2,0:T(1,128)S(1)}, u32[]{:S(2)}, u32[]{:S(2)}) async-start(s32[32,16,1]{1,2,0:T(1,128)} %bitcast.2), calls=%async_computation.1 | async-start | bytes 32768 | tf_op jit(solution)/shard_map/all_to_all | solution.py:155
  28.9 22.8 %copy-start.19 = (bf16[64,512]{1,0:T(8,128)(2,1)S(1)}, bf16[64,512]{1,0:T(8,128)(2,1)}, u32[]{:S(2)}) copy-start(bf16[64,512]{1,0:T(8,128)(2,1)} %param.22) | copy-start | bytes 196612
  28.9 22.8 %copy-start.20 = (bf16[64,512]{1,0:T(8,128)(2,1)S(1)}, bf16[64,512]{1,0:T(8,128)(2,1)}, u32[]{:S(2)}) copy-start(bf16[64,512]{1,0:T(8,128)(2,1)} %param.25) | copy-start | bytes 196612
  28.9 22.8 %copy-start.21 = (bf16[64,64]{1,0:T(8,128)(2,1)S(1)}, bf16[64,64]{1,0:T(8,128)(2,1)}, u32[]{:S(2)}) copy-start(bf16[64,64]{1,0:T(8,128)(2,1)} %param.23) | copy-start | bytes 24580
  28.9 22.8 %copy-start.22 = (bf16[64,64]{1,0:T(8,128)(2,1)S(1)}, bf16[64,64]{1,0:T(8,128)(2,1)}, u32[]{:S(2)}) copy-start(bf16[64,64]{1,0:T(8,128)(2,1)} %param.24) | copy-start | bytes 24580
  28.9 23.7 %copy-start.4 = (bf16[512,512]{1,0:T(8,128)(2,1)S(1)}, bf16[512,512]{1,0:T(8,128)(2,1)}, u32[]{:S(2)}) copy-start(bf16[512,512]{1,0:T(8,128)(2,1)} %param.18) | copy-start | bytes 1572868
  33.1 19.4 %copy-start.16 = (s32[32,16,1]{1,2,0:T(1,128)}, s32[32,16,1]{1,2,0:T(1,128)S(1)}, u32[]{:S(2)}) copy-start(s32[32,16,1]{1,2,0:T(1,128)S(1)} %all-to-all-done.1) | copy-start | bytes 6148
  33.1 15.9 %all-to-all-start = ((bf16[32,16,512]{2,1,0:T(8,128)(2,1)}), bf16[32,16,512]{2,1,0:T(8,128)(2,1)S(1)}, u32[]{:S(2)}, u32[]{:S(2)}) async-start(bf16[32,16,512]{2,1,0:T(8,128)(2,1)} %bitcast), calls=%async_computation | async-start | bytes 1048576 | tf_op jit(solution)/shard_map/all_to_all | solution.py:153
  37.3 42.7 %all-gather.11.cloned.1.call-start = ((), (), s32[]{:S(2)}) async-start(), calls=%async_computation.12 | async-start | bytes 2621440 | tf_op jit(solution)/shard_map/all_gather | solution.py:159
  51.6 78.8 %all-gather.7.cloned.1.call-start = ((), (), s32[]{:S(2)}) async-start(), calls=%async_computation.7 | async-start | bytes 4866048 | tf_op jit(solution)/shard_map/all_gather | solution.py:107
  52.5 306.3 %all-gather.13.cloned.1.call-start = ((), (), s32[]{:S(2)}) async-start(), calls=%async_computation.13 | async-start | bytes 2621440 | tf_op jit(solution)/shard_map/all_gather | solution.py:160
  54.5 18.1 %copy-start.13 = (bf16[64,1408]{1,0:T(8,128)(2,1)S(1)}, bf16[64,1408]{1,0:T(8,128)(2,1)}, u32[]{:S(2)}) copy-start(bf16[64,1408]{1,0:T(8,128)(2,1)} %param.29) | copy-start | bytes 540676
  54.5 18.1 %copy-start.14 = (bf16[64,1408]{1,0:T(8,128)(2,1)S(1)}, bf16[64,1408]{1,0:T(8,128)(2,1)}, u32[]{:S(2)}) copy-start(bf16[64,1408]{1,0:T(8,128)(2,1)} %param.28) | copy-start | bytes 540676
  54.5 18.1 %copy-start.15 = (bf16[64,1408]{1,0:T(8,128)(2,1)S(1)}, bf16[64,1408]{1,0:T(8,128)(2,1)}, u32[]{:S(2)}) copy-start(bf16[64,1408]{1,0:T(8,128)(2,1)} %param.27) | copy-start | bytes 540676
  54.5 19.2 %copy-start.26 = (s32[512]{0:T(512)S(1)}, s32[512]{0:T(512)}, u32[]{:S(2)}) copy-start(s32[512]{0:T(512)} %param.20) | copy-start | bytes 6148
  69.9 60.4 %copy-start.23 = (f32[2048]{0:T(1024)S(1)}, f32[2048]{0:T(1024)}, u32[]{:S(2)}) copy-start(f32[2048]{0:T(1024)} %param.21) | copy-start | bytes 24580
  72.5 286.2 %all-gather.9.cloned.1.call-start = ((), (), s32[]{:S(2)}) async-start(), calls=%async_computation.8 | async-start | bytes 17842176 | tf_op jit(solution)/shard_map/all_gather | solution.py:107
  73.5 410.4 %all-reduce.3.cloned.1.call-start = ((), (), s32[]{:S(2)}) async-start(), calls=%async_computation.10 | async-start | bytes 8388608 | tf_op jit(solution)/shard_map/psum | solution.py:225
  74.3 0.6 copy-start.30
  134.0 1.7 copy-start.5
  134.0 3.5 copy-start.31
  168.2 92.0 %collective-permute-start = (f32[512,2048]{1,0:T(8,128)S(1)}, f32[512,2048]{1,0:T(8,128)S(1)}, u32[]{:S(2)}, u32[]{:S(2)}) collective-permute-start(f32[512,2048]{1,0:T(8,128)S(1)} %fusion.63), channel_id=1, source_target_pairs={{0,1},{1,0},{2,3},{3,2},{4,5},{5,4},{6,7},{7,6},{8,9},{9,8},{10,11... | collective-permute-start | bytes 12582920 | tf_op jit(solution)/shard_map/ppermute | solution.py:18
  261.0 96.1 %copy-start.18 = (f32[2048]{0:T(1024)S(1)}, f32[2048]{0:T(1024)}, u32[]{:S(2)}) copy-start(f32[2048]{0:T(1024)} %param.26) | copy-start | bytes 24580
  261.0 92.8 %collective-permute-start.1 = (f32[512,2048]{1,0:T(8,128)S(1)}, f32[512,2048]{1,0:T(8,128)S(1)}, u32[]{:S(2)}, u32[]{:S(2)}) collective-permute-start(f32[512,2048]{1,0:T(8,128)S(1)} %add.146), channel_id=1, source_target_pairs={{0,2},{1,3},{2,0},{3,1},{4,6},{5,7},{6,4},{7,5},{8,10},{9,11},{10,... | collective-permute-start | bytes 12582920 | tf_op jit(solution)/shard_map/ppermute | solution.py:18
  354.9 2.1 copy-start.2
  358.7 6.6 copy-start.9
  358.7 8.9 copy-start.32
  380.0 5.4 copy-start.33
  390.5 246.8 %all-reduce.5.cloned.1.call-start = ((), (), s32[]{:S(2)}) async-start(), calls=%async_computation.11 | async-start | bytes 4194304 | tf_op jit(solution)/shard_map/psum | solution.py:261
  483.9 4.6 copy-start.3
  483.9 5.9 copy-start.6
  492.5 1.9 copy-start.7
  494.4 4.3 copy-start.27
  578.6 186.7 %reduce-scatter.5.cloned.1.call-start = ((), (), s32[]{:S(2)}) async-start(), calls=%async_computation.9 | async-start | bytes 2621440 | tf_op jit(solution)/shard_map/reduce_scatter | solution.py:212
  586.6 310.0 %reduce-scatter.7.cloned.1.call-start = ((), (), s32[]{:S(2)}) async-start(), calls=%async_computation.14 | async-start | bytes 23248896
  586.6 7.9 copy-start.10
  586.6 7.9 copy-start.35
  594.6 5.2 copy-start.11
  594.6 5.2 copy-start.34
  599.8 5.1 copy-start.24
  607.2 2.8 copy-start.8
  609.9 27.4 %copy-start.25 = (f32[2048]{0:T(1024)S(1)}, f32[2048]{0:T(1024)}, u32[]{:S(2)}) copy-start(f32[2048]{0:T(1024)} %param.21) | copy-start | bytes 24580
  612.6 30.9 %copy-start.12 = (bf16[2048,64]{0,1:T(8,128)(2,1)S(1)}, bf16[2048,64]{0,1:T(8,128)(2,1)}, u32[]{:S(2)}) copy-start(bf16[2048,64]{0,1:T(8,128)(2,1)} %convolution_convert_fusion.5) | copy-start | bytes 786436
  764.4 0.7 copy-start.17
  769.4 19.2 %all-to-all-start.2 = ((bf16[32,16,512]{2,1,0:T(8,128)(2,1)}), bf16[32,16,512]{2,1,0:T(8,128)(2,1)S(1)}, u32[]{:S(2)}, u32[]{:S(2)}) async-start(bf16[32,16,512]{2,1,0:T(8,128)(2,1)} %bitcast.14), calls=%async_computation.3 | async-start | bytes 1048576 | tf_op jit(solution)/shard_map/all_to_all | solution.py:289
  777.1 15.9 %copy-start.29 = (s32[512]{0:T(512)S(1)}, s32[512]{0:T(512)}, u32[]{:S(2)}) copy-start(s32[512]{0:T(512)} %copy-done.28) | copy-start | bytes 6148
  788.7 15.9 %all-to-all-start.4 = ((bf16[32,16,512]{2,1,0:T(8,128)(2,1)}), bf16[32,16,512]{2,1,0:T(8,128)(2,1)S(1)}, u32[]{:S(2)}, u32[]{:S(2)}) async-start(bf16[32,16,512]{2,1,0:T(8,128)(2,1)} %bitcast.24), calls=%async_computation.5 | async-start | bytes 1048576 | tf_op jit(solution)/shard_map/all_to_all | solution.py:290
  899.6 10.5 %copy-start.1 = (bf16[512,512]{1,0:T(8,128)(2,1)S(1)}, bf16[512,512]{1,0:T(8,128)(2,1)}, u32[]{:S(2)}) copy-start(bf16[512,512]{1,0:T(8,128)(2,1)} %param.17) | copy-start | bytes 1572868
Sparse Core Ops, SparseCore 0:
  51.7 28.2 all-gather.10
  82.8 47.4 all-gather.6
  132.6 29.6 all-gather.12
  164.4 74.3 all-gather.8
  390.6 93.2 all-reduce.2
  578.7 58.5 all-reduce.4
  639.7 29.5 reduce-scatter.4
  764.6 131.9 reduce-scatter.6
